TPU v7x, 32 devices: a whole 2x2x4 slice. The times are simulated.
32 devices in a mesh: seq: 2 (over x), book: 4 (over y, core), head: 4 (over z).
Axes of the slice: x: 2, y: 2, z: 4, core: 2. Of those that a mesh axis runs over, the one named last changes fastest.
Arguments:
- tokens: bfloat16 [4, 1024, 1024], P('book', 'seq'), may hold values from -40 to 40
- w_qkv: bfloat16 [1024, 3, 8, 128], P(None, None, 'head'), may hold values from -0.1875 to 0.1875
- w_out: bfloat16 [8, 128, 1024], P('head'), may hold values from -0.1875 to 0.1875
- slot_queries: bfloat16 [512, 8, 128], P(None, 'head'), may hold values from -40 to 40
- state_proj: bfloat16 [8, 128, 2, 128], P('head'), may hold values from -2.5 to 2.5
- init_state: float32 [4, 512, 8, 128], P('book', None, 'head'), may hold values from -6 to 6
- forget: float32 [4, 2, 8, 128], P('book', 'seq', 'head'), may hold values from 0.02 to 1
Outputs:
- mixed: bfloat16 [4, 1024, 1024], P('book', ('seq', 'head'))
- carried: float32 [4, 2, 512, 8, 128], P('book', 'seq', None, 'head')
All inputs are finite; a program needn't handle non-finite values.
Results may differ from a plain program's by a relative error of at most 0.03.
Values may be sent and summed in bfloat16 or wider, within the bound.
A program may use at most 64 MiB of HBM per device.

v0:
```python
import jax
import jax.numpy as jnp
from jax import lax
from jax.sharding import PartitionSpec as P

W = 512


def from_behind(block, axis, distance):
    devices = range(lax.axis_size(axis))
    route = [(i - distance, i) for i in devices if i - distance in devices]
    return lax.ppermute(block, axis, route)


def softmax_rows(scores):
    row_max = jnp.max(scores, axis=-1, keepdims=True)
    shifted = jnp.exp(scores - row_max)
    return shifted / jnp.sum(shifted, axis=-1, keepdims=True)


def local(tokens, w_qkv, w_out, slot_queries, state_proj, init_state, forget):
    tok_dev = tokens.shape[1]
    model_width = tokens.shape[2]
    head_count = w_qkv.shape[2]
    head_dim = w_qkv.shape[3]
    blocks_dev = tok_dev // W
    score_scale = head_dim ** (-0.5)
    projected = jnp.dot(
        tokens[0],
        w_qkv.reshape(model_width, 3 * head_count * head_dim),
        preferred_element_type=jnp.float32,
    )
    projected = projected.astype(jnp.bfloat16).reshape(tok_dev, 3, head_count, head_dim)
    query_rows = projected[:, 0]
    key_rows = projected[:, 1]
    value_rows = projected[:, 2]
    last_rows = jnp.stack([key_rows, value_rows], axis=0)
    before = from_behind(last_rows, "seq", 1)
    position = lax.axis_index("seq")
    retain = forget[0]
    slot_scores = (
        jnp.einsum("shd,khd->hsk", slot_queries, key_rows, preferred_element_type=jnp.float32)
        * score_scale
    )
    slot_weights = softmax_rows(slot_scores).astype(jnp.bfloat16)
    summaries = [
        jnp.einsum("hsk,khd->shd", slot_weights, value_rows, preferred_element_type=jnp.float32)
    ]
    decay_all = jnp.ones((head_count, head_dim), jnp.float32)
    offset = jnp.zeros(summaries[0].shape, jnp.float32)
    block_idx = 0
    decay_all = decay_all * retain[block_idx]
    offset = retain[block_idx] * offset + (1.0 - retain[block_idx]) * summaries[block_idx]
    initial = init_state[0]

    def relay_step(round_idx, current):
        passed = from_behind(decay_all * current + offset, "seq", 1)
        return jnp.where(position == 0, initial, passed)

    arriving_state = lax.fori_loop(0, lax.axis_size("seq") - 1, relay_step, initial)
    carry_state = arriving_state
    row_pos = jnp.arange(W, dtype=jnp.int32)[:, None]
    col_pos = jnp.arange(2 * W + slot_queries.shape[0], dtype=jnp.int32)[None, :]
    block_idx = 0
    prev_keys = before[0]
    prev_values = before[1]
    state_kv = jnp.einsum(
        "shd,hdce->sche",
        carry_state.astype(jnp.bfloat16),
        state_proj,
        preferred_element_type=jnp.float32,
    ).astype(jnp.bfloat16)
    key_all = jnp.concatenate([prev_keys, key_rows, state_kv[:, 0]], axis=0)
    value_all = jnp.concatenate([prev_values, value_rows, state_kv[:, 1]], axis=0)
    token_scores = (
        jnp.einsum("qhd,khd->hqk", query_rows, key_all, preferred_element_type=jnp.float32)
        * score_scale
    )
    global_block = position * blocks_dev + block_idx
    local_ok = (
        (col_pos - W <= row_pos) & (col_pos > row_pos) & ((col_pos >= W) | (global_block > 0))
    )
    allowed = jnp.where(col_pos < 2 * W, local_ok, True)
    token_scores = jnp.where(allowed[None], token_scores, -1e30)
    weights = softmax_rows(token_scores).astype(jnp.bfloat16)
    attended_blocks = jnp.einsum(
        "hqk,khd->qhd", weights, value_all, preferred_element_type=jnp.float32
    ).astype(jnp.bfloat16)
    carry_state = retain[block_idx] * carry_state + (1.0 - retain[block_idx]) * summaries[block_idx]
    carried_blocks = [carry_state]
    attended = attended_blocks.reshape(tok_dev, head_count * head_dim)
    w_flat = w_out.reshape(head_count * head_dim, model_width)
    row_share = tok_dev // lax.axis_size("head")
    partial_out = jnp.dot(attended, w_flat, preferred_element_type=jnp.float32)
    mixed_rows = lax.psum_scatter(partial_out, "head", scatter_dimension=0, tiled=True)
    mixed = mixed_rows.astype(jnp.bfloat16).reshape(1, row_share, model_width)
    carried = jnp.stack(carried_blocks, axis=0)[None]
    return (mixed, carried)


def solution(mesh):
    placed = (
        P("book", "seq", None),
        P(None, None, "head", None),
        P("head", None, None),
        P(None, "head", None),
        P("head", None, None, None),
        P("book", None, "head", None),
        P("book", "seq", "head", None),
    )
    return jax.shard_map(
        local,
        mesh=mesh,
        in_specs=placed,
        out_specs=(P("book", ("seq", "head"), None), P("book", "seq", None, "head", None)),
        check_vma=False,
    )
```

profile of v0, /device:TPU:0, one launch (start us, length us, event | category | flops | bytes accessed | tf_op | source)
XLA Modules:
  0.0 111.8 jit_solution(8904981238655243077)
XLA Ops:
  7.2 0.0 copy-start
  7.2 0.0 reduce-scatter.2.cloned.1.call-start
  7.2 4.0 %reshape.105 = bf16[1024,768]{1,0:T(8,128)(2,1)S(1)} reshape(bf16[1024,3,2,128]{3,2,1,0:T(2,128)(2,1)} %param.8) | data formatting | bytes 3145728 | tf_op jit(solution)/shard_map/reshape | solution.py:30
  11.2 0.0 copy-done
  11.2 1.0 convolution_convert_fusion
  12.2 0.2 reshape.106
  12.4 0.0 copy-start.5
  12.4 0.0 copy-start.2
  12.4 0.0 copy-start.3
  12.4 1.2 %fusion.53 = (bf16[512,1,2,128]{3,2,1,0:T(2,128)(2,1)}, bf16[512,1,2,128]{3,2,1,0:T(2,128)(2,1)S(1)}, bf16[512,1,2,128]{3,2,1,0:T(2,128)(2,1)S(1)}) fusion(bf16[512,3,2,128]{3,2,1,0:T(2,128)(2,1)S(1)} %reshape.106), kind=kLoop, calls=%fused_computation.73 | loop fusion | bytes 1572864 | tf_op jit(solution)/shard_map/slice | solution.py:34
  13.8 0.9 pad_maximum_fusion.1
  14.6 5.6 %collective-permute-start = (bf16[2,512,2,128]{3,1,2,0:T(8,128)(2,1)}, bf16[2,512,2,128]{3,1,2,0:T(8,128)(2,1)}, u32[]{:S(2)}, u32[]{:S(2)}) collective-permute-start(bf16[2,512,2,128]{3,1,2,0:T(8,128)(2,1)} %pad_maximum_fusion.1), channel_id=1, source_target_pairs={{0,16},{1,17},{2,18},{3,19},{4,20},{5,21},{6,22},{7,23},{8,24},{9,... | collective-permute-start | bytes 1572872 | tf_op jit(solution)/shard_map/ppermute | solution.py:12
  20.3 0.0 copy-done.5
  20.3 0.2 copy.11
  20.5 0.4 fusion.33
  20.9 1.3 %copy-done.1 = f32[2,512,512]{2,1,0:T(8,128)} copy-done((f32[2,512,512]{2,1,0:T(8,128)}, f32[2,512,512]{2,1,0:T(8,128)S(1)}, u32[]{:S(2)}) %copy-start.1) | copy-done | bytes 2097176
  22.3 0.6 fusion.54
  22.9 4.1 %fusion.30 = (f32[512,2,128]{0,2,1:T(8,128)}, f32[512,2,128]{0,2,1:T(8,128)}) fusion(f32[1,512,2,128]{1,3,2,0:T(8,128)S(1)} %copy.11, f32[2,128]{1,0:T(2,128)S(1)} %get-tuple-element.33, f32[2,128]{1,0:T(2,128)S(1)} %bitcast.91, f32[2,512]{1,0:T(2,128)S(1)} %fusion.54, f32[2,512,512]{2,1,0:T(8,128)} %copy-done.1, ...), kind=kOutput, calls=%fused_computation.41 | convolution fusion | flops 137364992 | bytes 3939328 | tf_op jit(solution)/shard_map/hsk,khd->shd/dot_general | solution.py:47
  27.0 1.3 %collective-permute-start.1 = (f32[512,2,128]{0,2,1:T(8,128)}, f32[512,2,128]{0,2,1:T(8,128)S(1)}, u32[]{:S(2)}, u32[]{:S(2)}) collective-permute-start(f32[512,2,128]{0,2,1:T(8,128)} %get-tuple-element.35), channel_id=1, source_target_pairs={{0,16},{1,17},{2,18},{3,19},{4,20},{5,21},{6,22},{7,23},{8,24},{9,... | collective-permute-start | bytes 1572872 | tf_op jit(solution)/shard_map/while/body/eval_jaxpr/ppermute | solution.py:12
  28.3 0.7 fusion.7
  29.0 13.2 %collective-permute-done.1 = f32[512,2,128]{0,2,1:T(8,128)S(1)} collective-permute-done((f32[512,2,128]{0,2,1:T(8,128)}, f32[512,2,128]{0,2,1:T(8,128)S(1)}, u32[]{:S(2)}, u32[]{:S(2)}) %collective-permute-start.1) | collective-permute-done | bytes 524320 | tf_op jit(solution)/shard_map/while/body/eval_jaxpr/ppermute | solution.py:12
  42.2 0.4 fusion.16
  42.5 0.8 slice_bitcast_fusion
  43.4 0.0 collective-permute-done
  43.4 1.9 %slice_bitcast_fusion.1 = (bf16[512,2,128]{2,0,1:T(8,128)(2,1)}, bf16[512,2,128]{2,0,1:T(8,128)(2,1)}) fusion(bf16[2,512,2,128]{3,1,2,0:T(8,128)(2,1)} %collective-permute-done), kind=kLoop, calls=%fused_computation.45 | loop fusion | bytes 1048576 | tf_op jit(solution)/shard_map/squeeze | solution.py:66
  45.3 6.1 %fusion.57 = (f32[2,512]{1,0:T(2,128)S(1)}, f32[2,512,1536]{2,1,0:T(8,128)}) fusion(pred[512,1536]{1,0:T(8,128)(4,1)S(1)} %fusion.7, bf16[512,2,128]{2,0,1:T(8,128)(2,1)} %get-tuple-element.28, bf16[512,2,128]{2,0,1:T(8,128)(2,1)S(1)} %bitcast.90, bf16[512,2,128]{2,0,1:T(8,128)(2,1)} %get-tuple-element.26, bf16[512,1,2,128]{3,2,1,0:T(2,128)(2,1)} %get-tuple-element.16), kind=kOutput, calls=%fused_computation.75 | convolution fusion | flops 411305472 | bytes 8130560 | tf_op jit(solution)/shard_map/sub | solution.py:17
  51.4 5.6 %convolution_bitcast_fusion = f32[512,1024]{1,0:T(8,128)} fusion(bf16[2,128,1024]{2,1,0:T(8,128)(2,1)} %param.9, f32[2,512,1536]{2,1,0:T(8,128)} %get-tuple-element.38, f32[2,512]{1,0:T(2,128)S(1)} %get-tuple-element.37, bf16[512,2,128]{2,0,1:T(8,128)(2,1)} %get-tuple-element.27, bf16[512,2,128]{2,0,1:T(8,128)(2,1)S(1)} %bitcast.88, ...), kind=kOutput, calls=%fused_computation.21 | convolution fusion | flops 676724736 | bytes 9703424 | tf_op jit(solution)/shard_map/dot_general | solution.py:94
  57.0 0.0 reduce-scatter.2.cloned.1.call-update
  57.1 1.2 %add_bitcast_fusion = f32[1,1,512,2,128]{2,4,3,1,0:T(8,128)S(1)} fusion(f32[512,2,128]{0,2,1:T(8,128)} %get-tuple-element.36, f32[2,128]{1,0:T(2,128)S(1)} %bitcast.92, f32[512,2,128]{0,2,1:T(8,128)S(1)} %collective-permute-done.1, f32[1,512,2,128]{1,3,2,0:T(8,128)S(1)} %copy.11, pred[]{:T(512)S(6)} %eq.4), kind=kLoop, calls=%fused_computation.42 | loop fusion | flops 393216 | bytes 2098177 | tf_op jit(solution)/shard_map/broadcast_in_dim;stack | solution.py:97
  58.2 1.0 copy.19
  59.2 44.0 %reduce-scatter.2.cloned.1.call-done = f32[128,1024]{1,0:T(8,128)} async-done(((f32[512,1024]{1,0:T(8,128)}), f32[128,1024]{1,0:T(8,128)}) %reduce-scatter.2.cloned.1.call-update) | async-done | bytes 524304 | tf_op jit(solution)/shard_map/reduce_scatter | solution.py:95
  103.2 1.8 %convert_bitcast_fusion = bf16[1,128,1024]{2,1,0:T(8,128)(2,1)} fusion(f32[128,1024]{1,0:T(8,128)} %reduce-scatter.2.cloned.1.call-done), kind=kLoop, calls=%fused_computation.52 | loop fusion | flops 131072 | bytes 786432 | tf_op jit(solution)/shard_map/reshape | solution.py:96
  (10 shorter events, 0.1 us)
Async XLA Ops:
  7.2 4.1 %copy-start = (bf16[1,512,1024]{2,1,0:T(8,128)(2,1)S(1)}, bf16[1,512,1024]{2,1,0:T(8,128)(2,1)}, u32[]{:S(2)}) copy-start(bf16[1,512,1024]{2,1,0:T(8,128)(2,1)} %param.7) | copy-start | bytes 3145732
  7.2 96.0 %reduce-scatter.2.cloned.1.call-start = ((), (), s32[]{:S(2)}) async-start(), calls=%async_computation.1 | async-start | bytes 2621440 | tf_op jit(solution)/shard_map/reduce_scatter | solution.py:95
  12.4 7.9 %copy-start.5 = (f32[1,1,2,128]{3,2,1,0:T(2,128)S(1)}, f32[1,1,2,128]{3,2,1,0:T(2,128)}, u32[]{:S(2)}) copy-start(f32[1,1,2,128]{3,2,1,0:T(2,128)} %param.13) | copy-start | bytes 3076
  12.4 7.9 %copy-start.2 = (f32[1,512,2,128]{3,2,1,0:T(2,128)S(1)}, f32[1,512,2,128]{3,2,1,0:T(2,128)}, u32[]{:S(2)}) copy-start(f32[1,512,2,128]{3,2,1,0:T(2,128)} %param.12) | copy-start | bytes 1572868
  12.4 8.1 %copy-start.3 = (bf16[512,2,128]{2,1,0:T(2,128)(2,1)S(1)}, bf16[512,2,128]{2,1,0:T(2,128)(2,1)}, u32[]{:S(2)}) copy-start(bf16[512,2,128]{2,1,0:T(2,128)(2,1)} %param.10) | copy-start | bytes 786436
  14.6 28.8 %collective-permute-start = (bf16[2,512,2,128]{3,1,2,0:T(8,128)(2,1)}, bf16[2,512,2,128]{3,1,2,0:T(8,128)(2,1)}, u32[]{:S(2)}, u32[]{:S(2)}) collective-permute-start(bf16[2,512,2,128]{3,1,2,0:T(8,128)(2,1)} %pad_maximum_fusion.1), channel_id=1, source_target_pairs={{0,16},{1,17},{2,18},{3,19},{4,20},{5,21},{6,22},{7,23},{8,24},{9,... | collective-permute-start | bytes 1572872 | tf_op jit(solution)/shard_map/ppermute | solution.py:12
  20.9 1.3 %copy-start.1 = (f32[2,512,512]{2,1,0:T(8,128)}, f32[2,512,512]{2,1,0:T(8,128)S(1)}, u32[]{:S(2)}) copy-start(f32[2,512,512]{2,1,0:T(8,128)S(1)} %fusion.33) | copy-start | bytes 6291460
  22.9 19.3 %copy-start.4 = (bf16[2,128,2,128]{3,2,1,0:T(2,128)(2,1)S(1)}, bf16[2,128,2,128]{3,2,1,0:T(2,128)(2,1)}, u32[]{:S(2)}) copy-start(bf16[2,128,2,128]{3,2,1,0:T(2,128)(2,1)} %param.11) | copy-start | bytes 393220
  27.0 15.2 %collective-permute-start.1 = (f32[512,2,128]{0,2,1:T(8,128)}, f32[512,2,128]{0,2,1:T(8,128)S(1)}, u32[]{:S(2)}, u32[]{:S(2)}) collective-permute-start(f32[512,2,128]{0,2,1:T(8,128)} %get-tuple-element.35), channel_id=1, source_target_pairs={{0,16},{1,17},{2,18},{3,19},{4,20},{5,21},{6,22},{7,23},{8,24},{9,... | collective-permute-start | bytes 1572872 | tf_op jit(solution)/shard_map/while/body/eval_jaxpr/ppermute | solution.py:12
Sparse Core Ops, SparseCore 0:
  57.2 45.9 reduce-scatter.1
where the time goes:
time: 112 us
  waiting for transfers between devices  57.2 us (51%)
  matrix products  17.6 us (16%)
  between operations  14.2 us (13%)
  local copies, waits for them, and re-layouts  10.8 us (10%)
  starting transfers between devices  6.98 us (6%)
  other arithmetic  5.09 us (5%)
    reduce_scatter x1, waiting for transfers between devices, local(): lax.psum_scatter(partial_out, 'head', scatter_dimension=0, tiled=True)  44 us
    ppermute x2, waiting for transfers between devices, from_behind(): return lax.ppermute(block, axis, route)  13.2 us
    ppermute x2, starting transfers between devices, from_behind(): return lax.ppermute(block, axis, route)  6.94 us
    sub x1, matrix products, softmax_rows(): shifted = jnp.exp(scores - row_max)  6.12 us
    dot_general x1, matrix products, local(): partial_out = jnp.dot(attended, w_flat, preferred_element_type=jnp.float32)  5.65 us
    dot_general x1, matrix products, local(): jnp.einsum('hsk,khd->shd', slot_weights, value_rows, preferred_element_ty...  4.09 us
    reshape x1, local copies, waits for them, and re-layouts, local(): w_qkv.reshape(model_width, 3 * head_count * head_dim)  3.99 us
    unnamed x16, local copies, waits for them, and re-layouts  2.65 us
  transfers between devices with their start and end apart: 3, of which 2 were waited for; matrix products, arithmetic and copies ran while one was open for 8% of the time, Pallas kernels for 0%

commit v1 on v0

--- a/solution.py
+++ b/solution.py
@@ -1,9 +1,318 @@
+import functools
 import jax
 import jax.numpy as jnp
 from jax import lax
+from jax.experimental import pallas as pl
+from jax.experimental.pallas import tpu as pltpu
 from jax.sharding import PartitionSpec as P
 
 W = 512
+MESH = pl.DeviceIdType.MESH
+F32 = jnp.float32
+BF16 = jnp.bfloat16
+
+
+def nt_dot(a, b):
+    return lax.dot_general(a, b, (((1,), (1,)), ((), ())), preferred_element_type=F32)
+
+
+def fused_kernel(
+    heads, tok_hbm, wqkv_hbm, wout_hbm, sq_hbm, sp_hbm, init_hbm, fg_hbm,
+    mixed_hbm, carried_hbm,
+    tok, wraw, wf, w2, sqraw, sqf, sqb, spraw, spf, init, fg, fg0,
+    kcat, vcat, qb, summ, state, skv, carried, wo, att, att_out, mixed,
+    in_sem, out_sem, kv_send, kv_recv, wz_send, wz_recv, wc_send, wc_recv, at_send, at_recv,
+):
+    seq = lax.axis_index("seq")
+    book = lax.axis_index("book")
+    head = lax.axis_index("head")
+    core = lax.rem(book, 2)
+    partner = book + 1 - 2 * core
+    hd = kcat.shape[2]
+    n_loc = kcat.shape[0]
+    slots = sqb.shape[1]
+    depth = tok.shape[1]
+    rows = att.shape[1]
+    half = wo.shape[1] // 2
+    scale = hd ** (-0.5)
+
+    loads = [
+        pltpu.make_async_copy(src, dst, in_sem.at[i])
+        for i, (src, dst) in enumerate(
+            [(wqkv_hbm, wraw), (tok_hbm, tok), (sq_hbm, sqraw), (init_hbm, init),
+             (fg_hbm, fg), (sp_hbm, spraw), (wout_hbm, wo.at[head])]
+        )
+    ]
+    for load in loads:
+        load.start()
+
+    barrier = pltpu.get_barrier_semaphore()
+    peers = [lax.rem(head + step, heads) for step in range(1, heads)]
+    for peer in peers:
+        pl.semaphore_signal(barrier, inc=1, device_id={"head": peer}, device_id_type=MESH)
+    pl.semaphore_signal(barrier, inc=1, device_id={"book": partner}, device_id_type=MESH)
+    pl.semaphore_signal(barrier, inc=1, device_id={"seq": 1 - seq}, device_id_type=MESH)
+    pl.semaphore_wait(barrier, heads + 1)
+
+    mine = pl.ds(pl.multiple_of(core * half, half), half)
+    wz = [
+        pltpu.make_async_remote_copy(
+            src_ref=wout_hbm.at[mine], dst_ref=wo.at[head, mine],
+            send_sem=wz_send.at[step], recv_sem=wz_recv.at[step],
+            device_id={"head": peer}, device_id_type=MESH,
+        )
+        for step, peer in enumerate(peers)
+    ]
+    wc = []
+    for step in range(heads - 1):
+        origin = lax.rem(head + heads - (step + 1), heads)
+        wc.append(
+            pltpu.make_async_remote_copy(
+                src_ref=wo.at[origin, mine], dst_ref=wo.at[origin, mine],
+                send_sem=wc_send.at[step], recv_sem=wc_recv.at[step],
+                device_id={"book": partner}, device_id_type=MESH,
+            )
+        )
+
+    def kv_copy(idx, src, dst):
+        return pltpu.make_async_remote_copy(
+            src_ref=src, dst_ref=dst, send_sem=kv_send.at[idx], recv_sem=kv_recv.at[idx],
+            device_id={"seq": 1 - seq}, device_id_type=MESH,
+        )
+
+    kv = [kv_copy(0, fg_hbm, fg0)]
+    for h in range(n_loc):
+        kv.append(kv_copy(1 + 2 * h, kcat.at[h, pl.ds(W, W)], kcat.at[h, pl.ds(0, W)]))
+        kv.append(kv_copy(2 + 2 * h, vcat.at[h, pl.ds(W, W)], vcat.at[h, pl.ds(0, W)]))
+
+    @pl.when(seq == 0)
+    def _():
+        kv[0].start()
+
+    for copy in wz:
+        copy.start()
+
+    loads[0].wait()
+    wf[...] = wraw[...].astype(F32)
+    period = 3 * n_loc
+
+    def project(part):
+        for h in range(n_loc):
+            w2[part, :, h * hd:(h + 1) * hd] = wf[
+                pl.ds(part * n_loc + h, depth, stride=period), :
+            ].astype(BF16)
+        return jnp.dot(tok[...], w2[part], preferred_element_type=F32).astype(BF16)
+
+    loads[1].wait()
+    keys = project(1)
+    for h in range(n_loc):
+        kcat[h, W:, :] = keys[:, h * hd:(h + 1) * hd]
+
+    @pl.when(seq == 0)
+    def _():
+        kv[1].start()
+
+    values = project(2)
+    for h in range(n_loc):
+        vcat[h, W:, :] = values[:, h * hd:(h + 1) * hd]
+
+    @pl.when(seq == 0)
+    def _():
+        for copy in kv[2:]:
+            copy.start()
+
+    queries = project(0)
+    for h in range(n_loc):
+        qb[h] = queries[:, h * hd:(h + 1) * hd]
+
+    loads[2].wait()
+    sqf[...] = sqraw[...].astype(F32)
+    for h in range(n_loc):
+        sqb[h] = sqf[pl.ds(h, slots, stride=n_loc), :].astype(BF16)
+    loads[5].wait()
+    spf[...] = spraw[...].astype(F32)
+    loads[3].wait()
+    loads[4].wait()
+
+    tile = 256
+
+    def slot_summary(h, row, off):
+        scores = nt_dot(sqb[h, row:row + tile, :], kcat[h, off:off + W, :])
+        top = jnp.max(scores, axis=1, keepdims=True)
+        p = jnp.exp((scores - top) * scale)
+        total = jnp.sum(p, axis=1, keepdims=True)
+        part = jnp.dot(p.astype(BF16), vcat[h, off:off + W, :], preferred_element_type=F32)
+        return part / total
+
+    for h in range(n_loc):
+        for row in range(0, slots, tile):
+            summ[h, row:row + tile, :] = slot_summary(h, row, W)
+
+    @pl.when(seq == 0)
+    def _():
+        for h in range(n_loc):
+            kcat[h, :W, :] = jnp.zeros((W, hd), BF16)
+            vcat[h, :W, :] = jnp.zeros((W, hd), BF16)
+            state[h] = init[pl.ds(h, slots, stride=n_loc), :]
+
+    @pl.when(seq == 1)
+    def _():
+        kv[0].wait_recv()
+        for h in range(n_loc):
+            kv[1 + 2 * h].wait_recv()
+            kv[2 + 2 * h].wait_recv()
+            keep = fg0[h:h + 1, :]
+            for row in range(0, slots, tile):
+                first = init[pl.ds(h + n_loc * row, tile, stride=n_loc), :]
+                state[h, row:row + tile, :] = keep * first + (1.0 - keep) * slot_summary(h, row, 0)
+
+    for h in range(n_loc):
+        keep = fg[h:h + 1, :]
+        base = h * 2 * hd
+        proj = jnp.concatenate(
+            [spf[pl.ds(base + c, hd, stride=2), :].astype(BF16) for c in range(2)], axis=1
+        )
+        skv[h] = jnp.dot(state[h].astype(BF16), proj, preferred_element_type=F32).astype(BF16)
+        carried[pl.ds(h, slots, stride=n_loc), :] = keep * state[h] + (1.0 - keep) * summ[h]
+    carried_out = pltpu.make_async_copy(carried, carried_hbm, out_sem.at[0])
+    carried_out.start()
+
+    span = W + rows
+    r_pos = lax.broadcasted_iota(jnp.int32, (rows, span), 0)
+    c_pos = lax.broadcasted_iota(jnp.int32, (rows, span), 1)
+    window = (c_pos > r_pos) & (c_pos <= r_pos + W)
+    floor = W * (1 - seq)
+
+    def attend(start, h):
+        q = qb[h, pl.ds(start, rows), :]
+        near = nt_dot(q, kcat[h, pl.ds(start, span), :])
+        allowed = window & (c_pos + start >= floor)
+        near = jnp.where(allowed, near, -1e30)
+        far = nt_dot(q, skv[h, :, :hd])
+        top = jnp.maximum(
+            jnp.max(near, axis=1, keepdims=True), jnp.max(far, axis=1, keepdims=True)
+        )
+        p_near = jnp.exp((near - top) * scale)
+        p_far = jnp.exp((far - top) * scale)
+        total = jnp.sum(p_near, axis=1, keepdims=True) + jnp.sum(p_far, axis=1, keepdims=True)
+        out = jnp.dot(
+            p_near.astype(BF16), vcat[h, pl.ds(start, span), :], preferred_element_type=F32
+        ) + jnp.dot(p_far.astype(BF16), skv[h, :, hd:], preferred_element_type=F32)
+        return (out / total).astype(BF16)
+
+    sends = []
+    for step in range(heads):
+        goal = lax.rem(head + step + 1, heads)
+        start = pl.multiple_of(goal * rows, rows)
+        for h in range(n_loc):
+            if step < heads - 1:
+                att_out[step, :, h * hd:(h + 1) * hd] = attend(start, h)
+            else:
+                att[head, :, h * hd:(h + 1) * hd] = attend(start, h)
+        if step < heads - 1:
+            copy = pltpu.make_async_remote_copy(
+                src_ref=att_out.at[step], dst_ref=att.at[head],
+                send_sem=at_send.at[step], recv_sem=at_recv.at[step],
+                device_id={"head": goal}, device_id_type=MESH,
+            )
+            copy.start()
+            sends.append(copy)
+
+    for step in range(heads - 1):
+        wz[step].wait_recv()
+        wc[step].start()
+
+    loads[6].wait()
+    acc = jnp.dot(att[head], wo[head], preferred_element_type=F32)
+    for step in range(heads - 1):
+        origin = lax.rem(head + heads - (step + 1), heads)
+        wc[step].wait_recv()
+        sends[step].wait_recv()
+        acc = acc + jnp.dot(att[origin], wo[origin], preferred_element_type=F32)
+    mixed[...] = acc.astype(BF16)
+    mixed_out = pltpu.make_async_copy(mixed, mixed_hbm, out_sem.at[1])
+    mixed_out.start()
+
+    for step in range(heads - 1):
+        wz[step].wait_send()
+        wc[step].wait_send()
+        sends[step].wait_send()
+
+    @pl.when(seq == 0)
+    def _():
+        for copy in kv:
+            copy.wait_send()
+
+    carried_out.wait()
+    mixed_out.wait()
+
+
+def fused_local(heads, tokens, w_qkv, w_out, slot_queries, state_proj, init_state, forget):
+    tok_dev, depth = tokens.shape[1:]
+    n_loc, hd = w_qkv.shape[2:]
+    slots = slot_queries.shape[0]
+    rows = tok_dev // heads
+    period = 3 * n_loc
+    anywhere = pl.BlockSpec(memory_space=pl.ANY)
+    v = pltpu.VMEM
+    dma = pltpu.SemaphoreType.DMA
+    mixed, carried = pl.pallas_call(
+        functools.partial(fused_kernel, heads),
+        out_shape=(
+            jax.ShapeDtypeStruct((rows, depth), BF16),
+            jax.ShapeDtypeStruct((slots * n_loc, hd), F32),
+        ),
+        in_specs=[anywhere] * 7,
+        out_specs=(anywhere, anywhere),
+        scratch_shapes=[
+            v((tok_dev, depth), BF16),
+            v((depth * period, hd), BF16),
+            v((depth * period, hd), F32),
+            v((3, depth, n_loc * hd), BF16),
+            v((slots * n_loc, hd), BF16),
+            v((slots * n_loc, hd), F32),
+            v((n_loc, slots, hd), BF16),
+            v((n_loc * hd * 2, hd), BF16),
+            v((n_loc * hd * 2, hd), F32),
+            v((slots * n_loc, hd), F32),
+            v((n_loc, hd), F32),
+            v((n_loc, hd), F32),
+            v((n_loc, 2 * W, hd), BF16),
+            v((n_loc, 2 * W, hd), BF16),
+            v((n_loc, tok_dev, hd), BF16),
+            v((n_loc, slots, hd), F32),
+            v((n_loc, slots, hd), F32),
+            v((n_loc, slots, 2 * hd), BF16),
+            v((slots * n_loc, hd), F32),
+            v((heads, n_loc * hd, depth), BF16),
+            v((heads, rows, n_loc * hd), BF16),
+            v((heads - 1, rows, n_loc * hd), BF16),
+            v((rows, depth), BF16),
+            dma((7,)),
+            dma((2,)),
+            dma((1 + 2 * n_loc,)),
+            dma((1 + 2 * n_loc,)),
+            dma((heads - 1,)),
+            dma((heads - 1,)),
+            dma((heads - 1,)),
+            dma((heads - 1,)),
+            dma((heads - 1,)),
+            dma((heads - 1,)),
+        ],
+        compiler_params=pltpu.CompilerParams(
+            collective_id=0, has_side_effects=True, vmem_limit_bytes=48 * 1024 * 1024
+        ),
+        name="fused_layer",
+    )(
+        tokens[0],
+        w_qkv.reshape(depth * period, hd),
+        w_out.reshape(n_loc * hd, depth),
+        slot_queries.reshape(slots * n_loc, hd),
+        state_proj.reshape(n_loc * hd * 2, hd),
+        init_state.reshape(slots * n_loc, hd),
+        forget.reshape(n_loc, hd),
+    )
+    return mixed.reshape(1, rows, depth), carried.reshape(1, 1, slots, n_loc, hd)
 
 
 def from_behind(block, axis, distance):
@@ -108,8 +417,9 @@
         P("book", None, "head", None),
         P("book", "seq", "head", None),
     )
+    body = functools.partial(fused_local, mesh.shape["head"]) if mesh.shape["seq"] == 2 else local
     return jax.shard_map(
-        local,
+        body,
         mesh=mesh,
         in_specs=placed,
         out_specs=(P("book", ("seq", "head"), None), P("book", "seq", None, "head", None)),

time: 112 us -> 44.4 us (0.40)
  waiting for transfers between devices: 57.2 us -> 0 us
  Pallas kernels: 0 us -> 34.7 us
  matrix products: 17.6 us -> 0 us
  between operations: 14.2 us -> 0.66 us
  starting transfers between devices: 6.98 us -> 0 us
  other arithmetic: 5.09 us -> 0 us
  local copies, waits for them, and re-layouts: 10.8 us -> 8.74 us
    reduce_scatter x1 -> x0, waiting for transfers between devices: 44 us -> none  [local(): lax.psum_scatter(partial_out, 'head', scatter_dimension=0, tiled=True)]
    pallas_call x0 -> x1, Pallas kernels: none -> 34.7 us  [fused_local(): pl.pallas_call(functools.partial(fused_kernel, heads), out_shape=(jax.Sha...]
    ppermute x2 -> x0, waiting for transfers between devices: 13.2 us -> none  [from_behind(): return lax.ppermute(block, axis, route)]
    dot_general x5 -> x0, matrix products: 11.5 us -> none  [the longest x1 5.65 us: local(): partial_out = jnp.dot(attended, w_flat, preferred_element_type=jnp.float32)]
    ppermute x2 -> x0, starting transfers between devices: 6.94 us -> none  [from_behind(): return lax.ppermute(block, axis, route)]
    sub x1 -> x0, matrix products: 6.12 us -> none  [softmax_rows(): shifted = jnp.exp(scores - row_max)]
    unnamed x16, local copies, waits for them, and re-layouts: 2.65 us -> 8.74 us
    reshape x2 -> x0, local copies, waits for them, and re-layouts: 4.17 us -> none  [the longest x1 3.99 us: local(): w_qkv.reshape(model_width, 3 * head_count * head_dim)]
  transfers between devices with their start and end apart: 3 -> 0, of which waited for: 2 -> 0; matrix products, arithmetic and copies ran while one was open for 8% -> 0% of each run, Pallas kernels for 0% -> 0%
where the time goes in v1:
time: 44.4 us; the launch traced here: 44.1 us
  Pallas kernels  34.7 us (78%)
  local copies, waits for them, and re-layouts  8.74 us (20%)
  between operations  0.66 us (1%)
    pallas_call x1, Pallas kernels, fused_local(): pl.pallas_call(functools.partial(fused_kernel, heads), out_shape=(jax.Sha...  34.7 us
    unnamed x16, local copies, waits for them, and re-layouts  8.74 us

profile of v1, /device:TPU:0, one launch (start us, length us, event | category | flops | bytes accessed | tf_op | source)
XLA Modules:
  0.0 44.1 jit_solution(11275083780353381529)
XLA Ops:
  0.6 0.0 copy-start
  0.6 1.4 %copy-done = bf16[1024,3,2,128]{3,2,1,0:T(2,128)(2,1)S(1)} copy-done((bf16[1024,3,2,128]{3,2,1,0:T(2,128)(2,1)S(1)}, bf16[1024,3,2,128]{3,2,1,0:T(2,128)(2,1)}, u32[]{:S(2)}) %copy-start) | copy-done | bytes 1572888
  2.0 0.0 copy-start.1
  2.0 1.2 %copy-done.1 = bf16[1,512,1024]{2,1,0:T(8,128)(2,1)S(1)} copy-done((bf16[1,512,1024]{2,1,0:T(8,128)(2,1)S(1)}, bf16[1,512,1024]{2,1,0:T(8,128)(2,1)}, u32[]{:S(2)}) %copy-start.1) | copy-done | bytes 1048600
  3.3 0.0 copy-start.2
  3.3 1.0 %copy-done.2 = bf16[2,128,1024]{2,1,0:T(8,128)(2,1)S(1)} copy-done((bf16[2,128,1024]{2,1,0:T(8,128)(2,1)S(1)}, bf16[2,128,1024]{2,1,0:T(8,128)(2,1)}, u32[]{:S(2)}) %copy-start.2) | copy-done | bytes 524312
  4.3 0.0 copy-start.3
  4.3 1.0 %copy-done.3 = f32[1,512,2,128]{3,2,1,0:T(2,128)S(1)} copy-done((f32[1,512,2,128]{3,2,1,0:T(2,128)S(1)}, f32[1,512,2,128]{3,2,1,0:T(2,128)}, u32[]{:S(2)}) %copy-start.3) | copy-done | bytes 524312
  5.4 0.0 copy-start.4
  5.4 0.9 %copy-done.4 = bf16[512,2,128]{2,1,0:T(2,128)(2,1)S(1)} copy-done((bf16[512,2,128]{2,1,0:T(2,128)(2,1)S(1)}, bf16[512,2,128]{2,1,0:T(2,128)(2,1)}, u32[]{:S(2)}) %copy-start.4) | copy-done | bytes 262168
  6.3 0.0 copy-start.5
  6.3 0.9 %copy-done.5 = bf16[2,128,2,128]{3,2,1,0:T(2,128)(2,1)S(1)} copy-done((bf16[2,128,2,128]{3,2,1,0:T(2,128)(2,1)S(1)}, bf16[2,128,2,128]{3,2,1,0:T(2,128)(2,1)}, u32[]{:S(2)}) %copy-start.5) | copy-done | bytes 131096
  7.2 0.0 copy-start.6
  7.2 0.7 %copy-done.6 = f32[1,1,2,128]{3,2,1,0:T(2,128)S(1)} copy-done((f32[1,1,2,128]{3,2,1,0:T(2,128)S(1)}, f32[1,1,2,128]{3,2,1,0:T(2,128)}, u32[]{:S(2)}) %copy-start.6) | copy-done | bytes 1048
  7.9 34.7 %fused_layer.1 = (bf16[128,1024]{1,0:T(8,128)(2,1)S(1)}, f32[1024,128]{1,0:T(8,128)S(1)}) custom-call(bf16[512,1024]{1,0:T(8,128)(2,1)S(1)} %bitcast.10, bf16[6144,128]{1,0:T(8,128)(2,1)S(1)} %bitcast.9, bf16[256,1024]{1,0:T(8,128)(2,1)S(1)} %bitcast.11, bf16[1024,128]{1,0:T(8,128)(2,1)S(1)} %bitcast.14, bf16[512,128]{1,0:T(8,128)(2,1)S(1)} %bitcast.16, ...), custom_call_target="tpu_custom_call" | custom-call | tf_op jit(solution)/shard_map/fused_layer/pallas_call | solution.py:259
  42.6 0.7 %copy.11 = bf16[1,128,1024]{2,1,0:T(8,128)(2,1)} copy(bf16[1,128,1024]{2,1,0:T(8,128)(2,1)S(1)} %bitcast.15) | data formatting | bytes 524288
  43.3 0.8 %copy.12 = f32[1,1,512,2,128]{4,3,2,1,0:T(2,128)} copy(f32[1,1,512,2,128]{4,3,2,1,0:T(2,128)S(1)} %bitcast.13) | data formatting | bytes 1048576
Async XLA Ops:
  0.6 1.4 %copy-start = (bf16[1024,3,2,128]{3,2,1,0:T(2,128)(2,1)S(1)}, bf16[1024,3,2,128]{3,2,1,0:T(2,128)(2,1)}, u32[]{:S(2)}) copy-start(bf16[1024,3,2,128]{3,2,1,0:T(2,128)(2,1)} %param.8) | copy-start | bytes 4718596
  2.0 1.2 %copy-start.1 = (bf16[1,512,1024]{2,1,0:T(8,128)(2,1)S(1)}, bf16[1,512,1024]{2,1,0:T(8,128)(2,1)}, u32[]{:S(2)}) copy-start(bf16[1,512,1024]{2,1,0:T(8,128)(2,1)} %param.7) | copy-start | bytes 3145732
  3.3 1.0 %copy-start.2 = (bf16[2,128,1024]{2,1,0:T(8,128)(2,1)S(1)}, bf16[2,128,1024]{2,1,0:T(8,128)(2,1)}, u32[]{:S(2)}) copy-start(bf16[2,128,1024]{2,1,0:T(8,128)(2,1)} %param.9) | copy-start | bytes 1572868
  4.3 1.0 %copy-start.3 = (f32[1,512,2,128]{3,2,1,0:T(2,128)S(1)}, f32[1,512,2,128]{3,2,1,0:T(2,128)}, u32[]{:S(2)}) copy-start(f32[1,512,2,128]{3,2,1,0:T(2,128)} %param.12) | copy-start | bytes 1572868
  5.4 0.9 %copy-start.4 = (bf16[512,2,128]{2,1,0:T(2,128)(2,1)S(1)}, bf16[512,2,128]{2,1,0:T(2,128)(2,1)}, u32[]{:S(2)}) copy-start(bf16[512,2,128]{2,1,0:T(2,128)(2,1)} %param.10) | copy-start | bytes 786436
  6.3 0.9 %copy-start.5 = (bf16[2,128,2,128]{3,2,1,0:T(2,128)(2,1)S(1)}, bf16[2,128,2,128]{3,2,1,0:T(2,128)(2,1)}, u32[]{:S(2)}) copy-start(bf16[2,128,2,128]{3,2,1,0:T(2,128)(2,1)} %param.11) | copy-start | bytes 393220
  7.2 0.7 %copy-start.6 = (f32[1,1,2,128]{3,2,1,0:T(2,128)S(1)}, f32[1,1,2,128]{3,2,1,0:T(2,128)}, u32[]{:S(2)}) copy-start(f32[1,1,2,128]{3,2,1,0:T(2,128)} %param.13) | copy-start | bytes 3076

commit v2 on v1

--- a/solution.py
+++ b/solution.py
@@ -20,27 +20,30 @@
     heads, tok_hbm, wqkv_hbm, wout_hbm, sq_hbm, sp_hbm, init_hbm, fg_hbm,
     mixed_hbm, carried_hbm,
     tok, wraw, wf, w2, sqraw, sqf, sqb, spraw, spf, init, fg, fg0,
-    kcat, vcat, qb, summ, state, skv, carried, wo, att, att_out, mixed,
-    in_sem, out_sem, kv_send, kv_recv, wz_send, wz_recv, wc_send, wc_recv, at_send, at_recv,
+    kcat, vcat, qb, summ, state, skv, own_acc, own_max, own_sum, carried, wo, att, att_out, mixed,
+    in_sem, out_sem, kv_send, kv_recv, wz_send, wz_recv, wy_send, wy_recv,
+    wc_send, wc_recv, wd_send, wd_recv, at_send, at_recv,
 ):
     seq = lax.axis_index("seq")
     book = lax.axis_index("book")
     head = lax.axis_index("head")
     core = lax.rem(book, 2)
-    partner = book + 1 - 2 * core
+    side = book // 2
+    core_mate = book + 1 - 2 * core
+    side_mate = lax.rem(book + 2, 4)
     hd = kcat.shape[2]
     n_loc = kcat.shape[0]
     slots = sqb.shape[1]
     depth = tok.shape[1]
-    rows = att.shape[1]
-    half = wo.shape[1] // 2
+    rows = att.shape[2]
+    part_rows = hd // 2
     scale = hd ** (-0.5)
 
     loads = [
         pltpu.make_async_copy(src, dst, in_sem.at[i])
         for i, (src, dst) in enumerate(
             [(wqkv_hbm, wraw), (tok_hbm, tok), (sq_hbm, sqraw), (init_hbm, init),
-             (fg_hbm, fg), (sp_hbm, spraw), (wout_hbm, wo.at[head])]
+             (fg_hbm, fg), (sp_hbm, spraw), (wout_hbm, wo.at[:, head])]
         )
     ]
     for load in loads:
@@ -48,80 +51,73 @@
 
     barrier = pltpu.get_barrier_semaphore()
     peers = [lax.rem(head + step, heads) for step in range(1, heads)]
+    origins = [lax.rem(head + heads - step, heads) for step in range(1, heads)]
     for peer in peers:
         pl.semaphore_signal(barrier, inc=1, device_id={"head": peer}, device_id_type=MESH)
-    pl.semaphore_signal(barrier, inc=1, device_id={"book": partner}, device_id_type=MESH)
+    pl.semaphore_signal(barrier, inc=1, device_id={"book": core_mate}, device_id_type=MESH)
+    pl.semaphore_signal(barrier, inc=1, device_id={"book": side_mate}, device_id_type=MESH)
     pl.semaphore_signal(barrier, inc=1, device_id={"seq": 1 - seq}, device_id_type=MESH)
-    pl.semaphore_wait(barrier, heads + 1)
-
-    mine = pl.ds(pl.multiple_of(core * half, half), half)
+
+    mine = pl.ds(pl.multiple_of(core * part_rows, part_rows), part_rows)
+
+    def remote(src, dst, send, recv, goal):
+        return pltpu.make_async_remote_copy(
+            src_ref=src, dst_ref=dst, send_sem=send, recv_sem=recv,
+            device_id=goal, device_id_type=MESH,
+        )
+
+    steps = range(heads - 1)
     wz = [
-        pltpu.make_async_remote_copy(
-            src_ref=wout_hbm.at[mine], dst_ref=wo.at[head, mine],
-            send_sem=wz_send.at[step], recv_sem=wz_recv.at[step],
-            device_id={"head": peer}, device_id_type=MESH,
-        )
-        for step, peer in enumerate(peers)
+        remote(wout_hbm.at[side, mine], wo.at[side, head, mine], wz_send.at[i], wz_recv.at[i],
+               {"head": peers[i]})
+        for i in steps
     ]
-    wc = []
-    for step in range(heads - 1):
-        origin = lax.rem(head + heads - (step + 1), heads)
-        wc.append(
-            pltpu.make_async_remote_copy(
-                src_ref=wo.at[origin, mine], dst_ref=wo.at[origin, mine],
-                send_sem=wc_send.at[step], recv_sem=wc_recv.at[step],
-                device_id={"book": partner}, device_id_type=MESH,
-            )
-        )
+    near = [wo.at[side, origins[i], mine] for i in steps]
+    across = [wo.at[1 - side, origins[i], mine] for i in steps]
+    wy = [remote(near[i], near[i], wy_send.at[i], wy_recv.at[i], {"book": side_mate}) for i in steps]
+    wc = [remote(near[i], near[i], wc_send.at[i], wc_recv.at[i], {"book": core_mate}) for i in steps]
+    wd = [
+        remote(across[i], across[i], wd_send.at[i], wd_recv.at[i], {"book": core_mate})
+        for i in steps
+    ]
 
     def kv_copy(idx, src, dst):
-        return pltpu.make_async_remote_copy(
-            src_ref=src, dst_ref=dst, send_sem=kv_send.at[idx], recv_sem=kv_recv.at[idx],
-            device_id={"seq": 1 - seq}, device_id_type=MESH,
-        )
+        return remote(src, dst, kv_send.at[idx], kv_recv.at[idx], {"seq": 1 - seq})
 
     kv = [kv_copy(0, fg_hbm, fg0)]
     for h in range(n_loc):
         kv.append(kv_copy(1 + 2 * h, kcat.at[h, pl.ds(W, W)], kcat.at[h, pl.ds(0, W)]))
         kv.append(kv_copy(2 + 2 * h, vcat.at[h, pl.ds(W, W)], vcat.at[h, pl.ds(0, W)]))
-
-    @pl.when(seq == 0)
-    def _():
-        kv[0].start()
-
-    for copy in wz:
-        copy.start()
 
     loads[0].wait()
     wf[...] = wraw[...].astype(F32)
     period = 3 * n_loc
 
-    def project(part):
-        for h in range(n_loc):
-            w2[part, :, h * hd:(h + 1) * hd] = wf[
-                pl.ds(part * n_loc + h, depth, stride=period), :
-            ].astype(BF16)
-        return jnp.dot(tok[...], w2[part], preferred_element_type=F32).astype(BF16)
+    def project(slot, columns):
+        for i, column in enumerate(columns):
+            w2[slot, :, i * hd:(i + 1) * hd] = wf[pl.ds(column, depth, stride=period), :].astype(BF16)
+        return jnp.dot(tok[...], w2[slot], preferred_element_type=F32).astype(BF16)
 
     loads[1].wait()
-    keys = project(1)
-    for h in range(n_loc):
-        kcat[h, W:, :] = keys[:, h * hd:(h + 1) * hd]
-
-    @pl.when(seq == 0)
-    def _():
-        kv[1].start()
-
-    values = project(2)
-    for h in range(n_loc):
-        vcat[h, W:, :] = values[:, h * hd:(h + 1) * hd]
-
-    @pl.when(seq == 0)
-    def _():
-        for copy in kv[2:]:
-            copy.start()
-
-    queries = project(0)
+    for h in range(n_loc):
+        both = project(h, (n_loc + h, 2 * n_loc + h))
+        kcat[h, W:, :] = both[:, :hd]
+        vcat[h, W:, :] = both[:, hd:]
+        if h == 0:
+            pl.semaphore_wait(barrier, heads + 2)
+
+        @pl.when(seq == 0)
+        def _():
+            kv[1 + 2 * h].start()
+            kv[2 + 2 * h].start()
+            if h == 0:
+                kv[0].start()
+
+        if h == 0:
+            for copy in wz:
+                copy.start()
+
+    queries = project(n_loc, range(n_loc))
     for h in range(n_loc):
         qb[h] = queries[:, h * hd:(h + 1) * hd]
 
@@ -148,17 +144,67 @@
         for row in range(0, slots, tile):
             summ[h, row:row + tile, :] = slot_summary(h, row, W)
 
-    @pl.when(seq == 0)
-    def _():
-        for h in range(n_loc):
-            kcat[h, :W, :] = jnp.zeros((W, hd), BF16)
-            vcat[h, :W, :] = jnp.zeros((W, hd), BF16)
+    r_pos = lax.broadcasted_iota(jnp.int32, (rows, rows), 0)
+    c_pos = lax.broadcasted_iota(jnp.int32, (rows, rows), 1)
+    causal = c_pos <= r_pos
+
+    def masked(scores, at, allowed):
+        blocks = [scores[:, c:c + rows] for c in range(0, scores.shape[1], rows)]
+        blocks[at] = jnp.where(allowed, blocks[at], -1e30)
+        return jnp.concatenate(blocks, axis=1)
+
+    for h in range(n_loc):
+        for i in range(heads):
+            q = qb[h, i * rows:(i + 1) * rows, :]
+            stop = W + (i + 1) * rows
+            scores = masked(nt_dot(q, kcat[h, W:stop, :]), i, causal)
+            top = jnp.max(scores, axis=1, keepdims=True)
+            p = jnp.exp((scores - top) * scale)
+            own_max[h, i] = top
+            own_sum[h, i] = jnp.sum(p, axis=1, keepdims=True)
+            own_acc[h, i] = jnp.dot(p.astype(BF16), vcat[h, W:stop, :], preferred_element_type=F32)
+
+    for i in steps:
+        wz[i].wait_recv()
+        wy[i].start()
+        wc[i].start()
+
+    def attend(h, i, with_prev):
+        q = qb[h, i * rows:(i + 1) * rows, :]
+        begin = i * rows
+        far = nt_dot(q, skv[h, :, :hd])
+        top = jnp.maximum(own_max[h, i], jnp.max(far, axis=1, keepdims=True))
+        if with_prev:
+            prev = masked(nt_dot(q, kcat[h, begin:W, :]), 0, jnp.logical_not(causal))
+            top = jnp.maximum(top, jnp.max(prev, axis=1, keepdims=True))
+        fade = jnp.exp((own_max[h, i] - top) * scale)
+        p_far = jnp.exp((far - top) * scale)
+        total = own_sum[h, i] * fade + jnp.sum(p_far, axis=1, keepdims=True)
+        out = own_acc[h, i] * fade + jnp.dot(
+            p_far.astype(BF16), skv[h, :, hd:], preferred_element_type=F32
+        )
+        if with_prev:
+            p_prev = jnp.exp((prev - top) * scale)
+            total = total + jnp.sum(p_prev, axis=1, keepdims=True)
+            out = out + jnp.dot(
+                p_prev.astype(BF16), vcat[h, begin:W, :], preferred_element_type=F32
+            )
+        att_out[h, i] = (out / total).astype(BF16)
+
+    def at_copy(h, step):
+        goal = lax.rem(head + step + 1, heads)
+        return remote(att_out.at[h, goal], att.at[h, head], at_send.at[h, step],
+                      at_recv.at[h, step], {"head": goal})
+
+    for h in range(n_loc):
+        @pl.when(seq == 0)
+        def _():
             state[h] = init[pl.ds(h, slots, stride=n_loc), :]
 
-    @pl.when(seq == 1)
-    def _():
-        kv[0].wait_recv()
-        for h in range(n_loc):
+        @pl.when(seq == 1)
+        def _():
+            if h == 0:
+                kv[0].wait_recv()
             kv[1 + 2 * h].wait_recv()
             kv[2 + 2 * h].wait_recv()
             keep = fg0[h:h + 1, :]
@@ -166,77 +212,55 @@
                 first = init[pl.ds(h + n_loc * row, tile, stride=n_loc), :]
                 state[h, row:row + tile, :] = keep * first + (1.0 - keep) * slot_summary(h, row, 0)
 
-    for h in range(n_loc):
-        keep = fg[h:h + 1, :]
         base = h * 2 * hd
         proj = jnp.concatenate(
             [spf[pl.ds(base + c, hd, stride=2), :].astype(BF16) for c in range(2)], axis=1
         )
         skv[h] = jnp.dot(state[h].astype(BF16), proj, preferred_element_type=F32).astype(BF16)
+
+        @pl.loop(0, heads)
+        def _(step):
+            goal = lax.rem(head + step + 1, heads)
+            for i in range(heads):
+                for s in range(2):
+                    @pl.when((goal == i) & (seq == s))
+                    def _():
+                        attend(h, i, s == 1)
+
+            @pl.when(step < heads - 1)
+            def _():
+                at_copy(h, step).start()
+
+        keep = fg[h:h + 1, :]
         carried[pl.ds(h, slots, stride=n_loc), :] = keep * state[h] + (1.0 - keep) * summ[h]
+        if h == 0:
+            for i in steps:
+                wy[i].wait_recv()
+                wd[i].start()
+
     carried_out = pltpu.make_async_copy(carried, carried_hbm, out_sem.at[0])
     carried_out.start()
 
-    span = W + rows
-    r_pos = lax.broadcasted_iota(jnp.int32, (rows, span), 0)
-    c_pos = lax.broadcasted_iota(jnp.int32, (rows, span), 1)
-    window = (c_pos > r_pos) & (c_pos <= r_pos + W)
-    floor = W * (1 - seq)
-
-    def attend(start, h):
-        q = qb[h, pl.ds(start, rows), :]
-        near = nt_dot(q, kcat[h, pl.ds(start, span), :])
-        allowed = window & (c_pos + start >= floor)
-        near = jnp.where(allowed, near, -1e30)
-        far = nt_dot(q, skv[h, :, :hd])
-        top = jnp.maximum(
-            jnp.max(near, axis=1, keepdims=True), jnp.max(far, axis=1, keepdims=True)
-        )
-        p_near = jnp.exp((near - top) * scale)
-        p_far = jnp.exp((far - top) * scale)
-        total = jnp.sum(p_near, axis=1, keepdims=True) + jnp.sum(p_far, axis=1, keepdims=True)
-        out = jnp.dot(
-            p_near.astype(BF16), vcat[h, pl.ds(start, span), :], preferred_element_type=F32
-        ) + jnp.dot(p_far.astype(BF16), skv[h, :, hd:], preferred_element_type=F32)
-        return (out / total).astype(BF16)
-
-    sends = []
-    for step in range(heads):
-        goal = lax.rem(head + step + 1, heads)
-        start = pl.multiple_of(goal * rows, rows)
-        for h in range(n_loc):
-            if step < heads - 1:
-                att_out[step, :, h * hd:(h + 1) * hd] = attend(start, h)
-            else:
-                att[head, :, h * hd:(h + 1) * hd] = attend(start, h)
-        if step < heads - 1:
-            copy = pltpu.make_async_remote_copy(
-                src_ref=att_out.at[step], dst_ref=att.at[head],
-                send_sem=at_send.at[step], recv_sem=at_recv.at[step],
-                device_id={"head": goal}, device_id_type=MESH,
-            )
-            copy.start()
-            sends.append(copy)
-
-    for step in range(heads - 1):
-        wz[step].wait_recv()
-        wc[step].start()
-
     loads[6].wait()
-    acc = jnp.dot(att[head], wo[head], preferred_element_type=F32)
-    for step in range(heads - 1):
-        origin = lax.rem(head + heads - (step + 1), heads)
-        wc[step].wait_recv()
-        sends[step].wait_recv()
-        acc = acc + jnp.dot(att[origin], wo[origin], preferred_element_type=F32)
+    for i in steps:
+        wc[i].wait_recv()
+        wd[i].wait_recv()
+    for h in range(n_loc):
+        att[h, head] = att_out[h, head]
+        for step in steps:
+            at_copy(h, step).wait_recv()
+        gathered = jnp.concatenate([att[h, o] for o in range(heads)], axis=1)
+        share = jnp.dot(gathered, wo[h].reshape(heads * hd, depth), preferred_element_type=F32)
+        acc = share if h == 0 else acc + share
     mixed[...] = acc.astype(BF16)
     mixed_out = pltpu.make_async_copy(mixed, mixed_hbm, out_sem.at[1])
     mixed_out.start()
 
-    for step in range(heads - 1):
-        wz[step].wait_send()
-        wc[step].wait_send()
-        sends[step].wait_send()
+    for i in steps:
+        for copy in (wz[i], wy[i], wc[i], wd[i]):
+            copy.wait_send()
+        for h in range(n_loc):
+            at_copy(h, i).wait_send()
 
     @pl.when(seq == 0)
     def _():
@@ -253,7 +277,7 @@
     slots = slot_queries.shape[0]
     rows = tok_dev // heads
     period = 3 * n_loc
-    anywhere = pl.BlockSpec(memory_space=pl.ANY)
+    anywhere = pl.BlockSpec(memory_space=pltpu.HBM)
     v = pltpu.VMEM
     dma = pltpu.SemaphoreType.DMA
     mixed, carried = pl.pallas_call(
@@ -283,30 +307,30 @@
             v((n_loc, slots, hd), F32),
             v((n_loc, slots, hd), F32),
             v((n_loc, slots, 2 * hd), BF16),
+            v((n_loc, heads, rows, hd), F32),
+            v((n_loc, heads, rows, 1), F32),
+            v((n_loc, heads, rows, 1), F32),
             v((slots * n_loc, hd), F32),
-            v((heads, n_loc * hd, depth), BF16),
-            v((heads, rows, n_loc * hd), BF16),
-            v((heads - 1, rows, n_loc * hd), BF16),
+            v((n_loc, heads, hd, depth), BF16),
+            v((n_loc, heads, rows, hd), BF16),
+            v((n_loc, heads, rows, hd), BF16),
             v((rows, depth), BF16),
             dma((7,)),
             dma((2,)),
             dma((1 + 2 * n_loc,)),
             dma((1 + 2 * n_loc,)),
-            dma((heads - 1,)),
-            dma((heads - 1,)),
-            dma((heads - 1,)),
-            dma((heads - 1,)),
-            dma((heads - 1,)),
-            dma((heads - 1,)),
+            *[dma((heads - 1,)) for _ in range(8)],
+            dma((n_loc, heads - 1)),
+            dma((n_loc, heads - 1)),
         ],
         compiler_params=pltpu.CompilerParams(
-            collective_id=0, has_side_effects=True, vmem_limit_bytes=48 * 1024 * 1024
+            collective_id=0, has_side_effects=True, vmem_limit_bytes=63 * 1024 * 1024
         ),
         name="fused_layer",
     )(
         tokens[0],
         w_qkv.reshape(depth * period, hd),
-        w_out.reshape(n_loc * hd, depth),
+        w_out,
         slot_queries.reshape(slots * n_loc, hd),
         state_proj.reshape(n_loc * hd * 2, hd),
         init_state.reshape(slots * n_loc, hd),
@@ -417,7 +441,8 @@
         P("book", None, "head", None),
         P("book", "seq", "head", None),
     )
-    body = functools.partial(fused_local, mesh.shape["head"]) if mesh.shape["seq"] == 2 else local
+    sizes = (mesh.shape["seq"], mesh.shape["book"], mesh.shape["head"])
+    body = functools.partial(fused_local, 4) if sizes == (2, 4, 4) else local
     return jax.shard_map(
         body,
         mesh=mesh,

time: 44.4 us -> 35.7 us (0.80)
  local copies, waits for them, and re-layouts: 8.74 us -> 3.54 us
  Pallas kernels: 34.7 us -> 31.4 us
    unnamed x16 -> x2, local copies, waits for them, and re-layouts: 8.74 us -> 3.54 us
    pallas_call x1, Pallas kernels: 34.7 us -> 31.4 us  [fused_local(): pl.pallas_call(functools.partial(fused_kernel, heads), out_shape=(jax.Sha...]
where the time goes in v2:
time: 35.7 us; the launch traced here: 35.5 us
  Pallas kernels  31.4 us (88%)
  local copies, waits for them, and re-layouts  3.54 us (10%)
  between operations  0.64 us (2%)
    pallas_call x1, Pallas kernels, fused_local(): pl.pallas_call(functools.partial(fused_kernel, heads), out_shape=(jax.Sha...  31.4 us
    unnamed x2, local copies, waits for them, and re-layouts  3.54 us

profile of v2, /device:TPU:0, one launch (start us, length us, event | category | flops | bytes accessed | tf_op | source)
XLA Modules:
  0.0 35.5 jit_solution(16088453618536259402)
XLA Ops:
  0.6 31.4 %fused_layer.1 = (bf16[128,1024]{1,0:T(8,128)(2,1)}, f32[1024,128]{1,0:T(8,128)}) custom-call(bf16[512,1024]{1,0:T(8,128)(2,1)} %bitcast.9, bf16[6144,128]{1,0:T(8,128)(2,1)} %bitcast.8, bf16[2,128,1024]{2,1,0:T(8,128)(2,1)} %wout_hbm.1, bf16[1024,128]{1,0:T(8,128)(2,1)} %bitcast.12, bf16[512,128]{1,0:T(8,128)(2,1)} %bitcast.14, f32[1024,128]{1,0:T(8,128)} %bitcast.10, ...), custom_call_target="tpu_custom_call" | custom-call | tf_op jit(solution)/shard_map/fused_layer/pallas_call | solution.py:283
  32.0 1.7 %copy.11 = bf16[1,128,1024]{2,1,0:T(8,128)(2,1)} copy(bf16[1,128,1024]{2,1,0:T(8,128)(2,1)} %bitcast.13) | data formatting | bytes 524288
  33.7 1.9 %copy.12 = f32[1,1,512,2,128]{4,3,2,1,0:T(2,128)} copy(f32[1,1,512,2,128]{4,3,2,1,0:T(2,128)} %bitcast.11) | data formatting | bytes 1048576

commit v3 on v2

--- a/solution.py
+++ b/solution.py
@@ -21,7 +21,7 @@
     mixed_hbm, carried_hbm,
     tok, wraw, wf, w2, sqraw, sqf, sqb, spraw, spf, init, fg, fg0,
     kcat, vcat, qb, summ, state, skv, own_acc, own_max, own_sum, carried, wo, att, att_out, mixed,
-    in_sem, out_sem, kv_send, kv_recv, wz_send, wz_recv, wy_send, wy_recv,
+    in_sem, w_sem, out_sem, kv_send, kv_recv, wz_send, wz_recv, wy_send, wy_recv,
     wc_send, wc_recv, wd_send, wd_recv, at_send, at_recv,
 ):
     seq = lax.axis_index("seq")
@@ -42,16 +42,22 @@
     loads = [
         pltpu.make_async_copy(src, dst, in_sem.at[i])
         for i, (src, dst) in enumerate(
-            [(wqkv_hbm, wraw), (tok_hbm, tok), (sq_hbm, sqraw), (init_hbm, init),
+            [(tok_hbm, tok), (sq_hbm, sqraw), (init_hbm, init),
              (fg_hbm, fg), (sp_hbm, spraw), (wout_hbm, wo.at[:, head])]
         )
     ]
+    pieces = [pl.ds(i * wraw.shape[0] // 4, wraw.shape[0] // 4) for i in range(4)]
+    weights = [
+        pltpu.make_async_copy(wqkv_hbm.at[piece], wraw.at[piece], w_sem.at[i])
+        for i, piece in enumerate(pieces)
+    ]
+    for load in weights:
+        load.start()
     for load in loads:
         load.start()
 
     barrier = pltpu.get_barrier_semaphore()
-    peers = [lax.rem(head + step, heads) for step in range(1, heads)]
-    origins = [lax.rem(head + heads - step, heads) for step in range(1, heads)]
+    peers = [head + 1 - 2 * lax.rem(head, 2), lax.rem(head + 2, 4), 3 - head]
     for peer in peers:
         pl.semaphore_signal(barrier, inc=1, device_id={"head": peer}, device_id_type=MESH)
     pl.semaphore_signal(barrier, inc=1, device_id={"book": core_mate}, device_id_type=MESH)
@@ -66,20 +72,24 @@
             device_id=goal, device_id_type=MESH,
         )
 
-    steps = range(heads - 1)
-    wz = [
-        remote(wout_hbm.at[side, mine], wo.at[side, head, mine], wz_send.at[i], wz_recv.at[i],
-               {"head": peers[i]})
-        for i in steps
+    wz = [remote(wout_hbm.at[:, mine], wo.at[:, head, mine], wz_send.at[0], wz_recv.at[0],
+                 {"head": peers[0]})]
+    near = [wo.at[:, peers[0], mine]]
+    for i in (1, 2):
+        wz.append(remote(wout_hbm.at[side, mine], wo.at[side, head, mine], wz_send.at[i],
+                         wz_recv.at[i], {"head": peers[i]}))
+        near.append(wo.at[side, peers[i], mine])
+    wc = [
+        remote(near[i], near[i], wc_send.at[i], wc_recv.at[i], {"book": core_mate})
+        for i in range(3)
     ]
-    near = [wo.at[side, origins[i], mine] for i in steps]
-    across = [wo.at[1 - side, origins[i], mine] for i in steps]
-    wy = [remote(near[i], near[i], wy_send.at[i], wy_recv.at[i], {"book": side_mate}) for i in steps]
-    wc = [remote(near[i], near[i], wc_send.at[i], wc_recv.at[i], {"book": core_mate}) for i in steps]
-    wd = [
-        remote(across[i], across[i], wd_send.at[i], wd_recv.at[i], {"book": core_mate})
-        for i in steps
-    ]
+    wy, wd = [], []
+    for i in (1, 2):
+        across = wo.at[1 - side, peers[i], mine]
+        wy.append(remote(near[i], near[i], wy_send.at[i - 1], wy_recv.at[i - 1],
+                         {"book": side_mate}))
+        wd.append(remote(across, across, wd_send.at[i - 1], wd_recv.at[i - 1],
+                         {"book": core_mate}))
 
     def kv_copy(idx, src, dst):
         return remote(src, dst, kv_send.at[idx], kv_recv.at[idx], {"seq": 1 - seq})
@@ -89,8 +99,13 @@
         kv.append(kv_copy(1 + 2 * h, kcat.at[h, pl.ds(W, W)], kcat.at[h, pl.ds(0, W)]))
         kv.append(kv_copy(2 + 2 * h, vcat.at[h, pl.ds(W, W)], vcat.at[h, pl.ds(0, W)]))
 
-    loads[0].wait()
-    wf[...] = wraw[...].astype(F32)
+    pl.semaphore_wait(barrier, heads + 2)
+    for copy in wz:
+        copy.start()
+
+    for load, piece in zip(weights, pieces):
+        load.wait()
+        wf[piece, :] = wraw[piece, :].astype(F32)
     period = 3 * n_loc
 
     def project(slot, columns):
@@ -98,13 +113,11 @@
             w2[slot, :, i * hd:(i + 1) * hd] = wf[pl.ds(column, depth, stride=period), :].astype(BF16)
         return jnp.dot(tok[...], w2[slot], preferred_element_type=F32).astype(BF16)
 
-    loads[1].wait()
+    loads[0].wait()
     for h in range(n_loc):
         both = project(h, (n_loc + h, 2 * n_loc + h))
         kcat[h, W:, :] = both[:, :hd]
         vcat[h, W:, :] = both[:, hd:]
-        if h == 0:
-            pl.semaphore_wait(barrier, heads + 2)
 
         @pl.when(seq == 0)
         def _():
@@ -113,22 +126,21 @@
             if h == 0:
                 kv[0].start()
 
-        if h == 0:
-            for copy in wz:
-                copy.start()
-
     queries = project(n_loc, range(n_loc))
     for h in range(n_loc):
         qb[h] = queries[:, h * hd:(h + 1) * hd]
 
+    wz[0].wait_recv()
+    wc[0].start()
+
+    loads[1].wait()
+    sqf[...] = sqraw[...].astype(F32)
+    for h in range(n_loc):
+        sqb[h] = sqf[pl.ds(h, slots, stride=n_loc), :].astype(BF16)
+    loads[4].wait()
+    spf[...] = spraw[...].astype(F32)
     loads[2].wait()
-    sqf[...] = sqraw[...].astype(F32)
-    for h in range(n_loc):
-        sqb[h] = sqf[pl.ds(h, slots, stride=n_loc), :].astype(BF16)
-    loads[5].wait()
-    spf[...] = spraw[...].astype(F32)
     loads[3].wait()
-    loads[4].wait()
 
     tile = 256
 
@@ -164,9 +176,9 @@
             own_sum[h, i] = jnp.sum(p, axis=1, keepdims=True)
             own_acc[h, i] = jnp.dot(p.astype(BF16), vcat[h, W:stop, :], preferred_element_type=F32)
 
-    for i in steps:
+    for i in (1, 2):
         wz[i].wait_recv()
-        wy[i].start()
+        wy[i - 1].start()
         wc[i].start()
 
     def attend(h, i, with_prev):
@@ -191,10 +203,13 @@
             )
         att_out[h, i] = (out / total).astype(BF16)
 
-    def at_copy(h, step):
-        goal = lax.rem(head + step + 1, heads)
-        return remote(att_out.at[h, goal], att.at[h, head], at_send.at[h, step],
-                      at_recv.at[h, step], {"head": goal})
+    def at_copy(h, goal):
+        return remote(att_out.at[h, goal], att.at[h, head], at_send.at[h, goal],
+                      at_recv.at[h, head], {"head": goal})
+
+    def at_arrival(h, origin):
+        return remote(att_out.at[h, origin], att.at[h, origin], at_send.at[h, origin],
+                      at_recv.at[h, origin], {"head": origin})
 
     for h in range(n_loc):
         @pl.when(seq == 0)
@@ -218,37 +233,35 @@
         )
         skv[h] = jnp.dot(state[h].astype(BF16), proj, preferred_element_type=F32).astype(BF16)
 
-        @pl.loop(0, heads)
-        def _(step):
-            goal = lax.rem(head + step + 1, heads)
-            for i in range(heads):
-                for s in range(2):
-                    @pl.when((goal == i) & (seq == s))
-                    def _():
+        for group in ((0, 2), (1, 3)):
+            for s in range(2):
+                @pl.when(seq == s)
+                def _():
+                    for i in group:
                         attend(h, i, s == 1)
 
-            @pl.when(step < heads - 1)
-            def _():
-                at_copy(h, step).start()
+            for i in group:
+                @pl.when(head != i)
+                def _():
+                    at_copy(h, i).start()
 
         keep = fg[h:h + 1, :]
         carried[pl.ds(h, slots, stride=n_loc), :] = keep * state[h] + (1.0 - keep) * summ[h]
         if h == 0:
-            for i in steps:
+            for i in range(2):
                 wy[i].wait_recv()
                 wd[i].start()
 
     carried_out = pltpu.make_async_copy(carried, carried_hbm, out_sem.at[0])
     carried_out.start()
 
-    loads[6].wait()
-    for i in steps:
-        wc[i].wait_recv()
-        wd[i].wait_recv()
+    loads[5].wait()
+    for copy in wc + wd:
+        copy.wait_recv()
     for h in range(n_loc):
         att[h, head] = att_out[h, head]
-        for step in steps:
-            at_copy(h, step).wait_recv()
+        for peer in peers:
+            at_arrival(h, peer).wait_recv()
         gathered = jnp.concatenate([att[h, o] for o in range(heads)], axis=1)
         share = jnp.dot(gathered, wo[h].reshape(heads * hd, depth), preferred_element_type=F32)
         acc = share if h == 0 else acc + share
@@ -256,11 +269,11 @@
     mixed_out = pltpu.make_async_copy(mixed, mixed_hbm, out_sem.at[1])
     mixed_out.start()
 
-    for i in steps:
-        for copy in (wz[i], wy[i], wc[i], wd[i]):
-            copy.wait_send()
-        for h in range(n_loc):
-            at_copy(h, i).wait_send()
+    for copy in wz + wy + wc + wd:
+        copy.wait_send()
+    for h in range(n_loc):
+        for peer in peers:
+            at_copy(h, peer).wait_send()
 
     @pl.when(seq == 0)
     def _():
@@ -287,7 +300,7 @@
             jax.ShapeDtypeStruct((slots * n_loc, hd), F32),
         ),
         in_specs=[anywhere] * 7,
-        out_specs=(anywhere, anywhere),
+        out_specs=[pl.BlockSpec(memory_space=pl.ANY)] * 2,
         scratch_shapes=[
             v((tok_dev, depth), BF16),
             v((depth * period, hd), BF16),
@@ -315,27 +328,31 @@
             v((n_loc, heads, rows, hd), BF16),
             v((n_loc, heads, rows, hd), BF16),
             v((rows, depth), BF16),
-            dma((7,)),
+            dma((6,)),
+            dma((4,)),
             dma((2,)),
             dma((1 + 2 * n_loc,)),
             dma((1 + 2 * n_loc,)),
             *[dma((heads - 1,)) for _ in range(8)],
-            dma((n_loc, heads - 1)),
-            dma((n_loc, heads - 1)),
+            dma((n_loc, heads)),
+            dma((n_loc, heads)),
         ],
         compiler_params=pltpu.CompilerParams(
-            collective_id=0, has_side_effects=True, vmem_limit_bytes=63 * 1024 * 1024
+            collective_id=0, has_side_effects=True, vmem_limit_bytes=48 * 1024 * 1024
         ),
         name="fused_layer",
-    )(
-        tokens[0],
-        w_qkv.reshape(depth * period, hd),
-        w_out,
-        slot_queries.reshape(slots * n_loc, hd),
-        state_proj.reshape(n_loc * hd * 2, hd),
-        init_state.reshape(slots * n_loc, hd),
-        forget.reshape(n_loc, hd),
-    )
+    )(*[
+        pltpu.with_memory_space_constraint(operand, pltpu.HBM)
+        for operand in (
+            tokens[0],
+            w_qkv.reshape(depth * period, hd),
+            w_out,
+            slot_queries.reshape(slots * n_loc, hd),
+            state_proj.reshape(n_loc * hd * 2, hd),
+            init_state.reshape(slots * n_loc, hd),
+            forget.reshape(n_loc, hd),
+        )
+    ])
     return mixed.reshape(1, rows, depth), carried.reshape(1, 1, slots, n_loc, hd)
 
 

time: 35.7 us -> 33.6 us (0.941)
  the two profiles are of different devices: /device:TPU:0 before, /device:TPU:26 now
where the time goes in v3:
time: 33.6 us; the launch traced here: 33.4 us
  Pallas kernels  31.3 us (93%)
  local copies, waits for them, and re-layouts  1.5 us (4%)
  between operations  0.64 us (2%)
    pallas_call x1, Pallas kernels, fused_local(): pl.pallas_call(functools.partial(fused_kernel, heads), out_shape=(jax.Sha...  31.3 us
    unnamed x2, local copies, waits for them, and re-layouts  1.5 us

profile of v3, /device:TPU:26, one launch (start us, length us, event | category | flops | bytes accessed | tf_op | source)
XLA Modules:
  0.0 33.4 jit_solution(5112125792256595067)
XLA Ops:
  0.6 31.3 %fused_layer.1 = (bf16[128,1024]{1,0:T(8,128)(2,1)S(1)}, f32[1024,128]{1,0:T(8,128)S(1)}) custom-call(bf16[512,1024]{1,0:T(8,128)(2,1)} %bitcast.11, bf16[6144,128]{1,0:T(8,128)(2,1)} %bitcast.10, bf16[2,128,1024]{2,1,0:T(8,128)(2,1)} %wout_hbm.1, bf16[1024,128]{1,0:T(8,128)(2,1)} %bitcast.13, bf16[512,128]{1,0:T(8,128)(2,1)} %bitcast.14, ...), custom_call_target="tpu_custom_call" | custom-call | tf_op jit(solution)/shard_map/fused_layer/pallas_call | solution.py:296
  31.9 0.7 %copy.11 = bf16[1,128,1024]{2,1,0:T(8,128)(2,1)} copy(bf16[1,128,1024]{2,1,0:T(8,128)(2,1)S(1)} %bitcast.9) | data formatting | bytes 524288
  32.6 0.8 %copy.12 = f32[1,1,512,2,128]{4,3,2,1,0:T(2,128)} copy(f32[1,1,512,2,128]{4,3,2,1,0:T(2,128)S(1)} %bitcast.8) | data formatting | bytes 1048576

commit v4 on v3

--- a/solution.py
+++ b/solution.py
@@ -176,11 +176,6 @@
             own_sum[h, i] = jnp.sum(p, axis=1, keepdims=True)
             own_acc[h, i] = jnp.dot(p.astype(BF16), vcat[h, W:stop, :], preferred_element_type=F32)
 
-    for i in (1, 2):
-        wz[i].wait_recv()
-        wy[i - 1].start()
-        wc[i].start()
-
     def attend(h, i, with_prev):
         q = qb[h, i * rows:(i + 1) * rows, :]
         begin = i * rows
@@ -233,6 +228,12 @@
         )
         skv[h] = jnp.dot(state[h].astype(BF16), proj, preferred_element_type=F32).astype(BF16)
 
+        if h == 0:
+            for i in (1, 2):
+                wz[i].wait_recv()
+                wy[i - 1].start()
+                wc[i].start()
+
         for group in ((0, 2), (1, 3)):
             for s in range(2):
                 @pl.when(seq == s)
@@ -247,7 +248,7 @@
 
         keep = fg[h:h + 1, :]
         carried[pl.ds(h, slots, stride=n_loc), :] = keep * state[h] + (1.0 - keep) * summ[h]
-        if h == 0:
+        if h == n_loc - 1:
             for i in range(2):
                 wy[i].wait_recv()
                 wd[i].start()

time: 33.6 us -> 30.6 us (0.911)
  the two profiles are of different devices: /device:TPU:26 before, /device:TPU:3 now
where the time goes in v4:
time: 30.6 us; the launch traced here: 30.5 us
  Pallas kernels  28.3 us (92%)
  local copies, waits for them, and re-layouts  1.5 us (5%)
  between operations  0.64 us (2%)
    pallas_call x1, Pallas kernels, fused_local(): pl.pallas_call(functools.partial(fused_kernel, heads), out_shape=(jax.Sha...  28.3 us
    unnamed x2, local copies, waits for them, and re-layouts  1.5 us

profile of v4, /device:TPU:3, one launch (start us, length us, event | category | flops | bytes accessed | tf_op | source)
XLA Modules:
  0.0 30.5 jit_solution(826447608589855484)
XLA Ops:
  0.6 28.3 %fused_layer.1 = (bf16[128,1024]{1,0:T(8,128)(2,1)S(1)}, f32[1024,128]{1,0:T(8,128)S(1)}) custom-call(bf16[512,1024]{1,0:T(8,128)(2,1)} %bitcast.11, bf16[6144,128]{1,0:T(8,128)(2,1)} %bitcast.10, bf16[2,128,1024]{2,1,0:T(8,128)(2,1)} %wout_hbm.1, bf16[1024,128]{1,0:T(8,128)(2,1)} %bitcast.13, bf16[512,128]{1,0:T(8,128)(2,1)} %bitcast.14, ...), custom_call_target="tpu_custom_call" | custom-call | tf_op jit(solution)/shard_map/fused_layer/pallas_call | solution.py:297
  29.0 0.7 %copy.11 = bf16[1,128,1024]{2,1,0:T(8,128)(2,1)} copy(bf16[1,128,1024]{2,1,0:T(8,128)(2,1)S(1)} %bitcast.9) | data formatting | bytes 524288
  29.7 0.8 %copy.12 = f32[1,1,512,2,128]{4,3,2,1,0:T(2,128)} copy(f32[1,1,512,2,128]{4,3,2,1,0:T(2,128)S(1)} %bitcast.8) | data formatting | bytes 1048576

commit v5 on v4

--- a/solution.py
+++ b/solution.py
@@ -228,12 +228,6 @@
         )
         skv[h] = jnp.dot(state[h].astype(BF16), proj, preferred_element_type=F32).astype(BF16)
 
-        if h == 0:
-            for i in (1, 2):
-                wz[i].wait_recv()
-                wy[i - 1].start()
-                wc[i].start()
-
         for group in ((0, 2), (1, 3)):
             for s in range(2):
                 @pl.when(seq == s)
@@ -245,6 +239,12 @@
                 @pl.when(head != i)
                 def _():
                     at_copy(h, i).start()
+
+        if h == 0:
+            for i in (1, 2):
+                wz[i].wait_recv()
+                wy[i - 1].start()
+                wc[i].start()
 
         keep = fg[h:h + 1, :]
         carried[pl.ds(h, slots, stride=n_loc), :] = keep * state[h] + (1.0 - keep) * summ[h]

time: 30.6 us -> 32.7 us (1.069)
  Pallas kernels: 28.3 us -> 30.5 us
    pallas_call x1, Pallas kernels: 28.3 us -> 30.5 us  [fused_local(): pl.pallas_call(functools.partial(fused_kernel, heads), out_shape=(jax.Sha...]
where the time goes in v5:
time: 32.7 us; the launch traced here: 32.6 us
  Pallas kernels  30.5 us (93%)
  local copies, waits for them, and re-layouts  1.5 us (5%)
  between operations  0.64 us (2%)
    pallas_call x1, Pallas kernels, fused_local(): pl.pallas_call(functools.partial(fused_kernel, heads), out_shape=(jax.Sha...  30.5 us
    unnamed x2, local copies, waits for them, and re-layouts  1.5 us

profile of v5, /device:TPU:3, one launch (start us, length us, event | category | flops | bytes accessed | tf_op | source)
XLA Modules:
  0.0 32.6 jit_solution(752971830359968832)
XLA Ops:
  0.6 30.5 %fused_layer.1 = (bf16[128,1024]{1,0:T(8,128)(2,1)S(1)}, f32[1024,128]{1,0:T(8,128)S(1)}) custom-call(bf16[512,1024]{1,0:T(8,128)(2,1)} %bitcast.11, bf16[6144,128]{1,0:T(8,128)(2,1)} %bitcast.10, bf16[2,128,1024]{2,1,0:T(8,128)(2,1)} %wout_hbm.1, bf16[1024,128]{1,0:T(8,128)(2,1)} %bitcast.13, bf16[512,128]{1,0:T(8,128)(2,1)} %bitcast.14, ...), custom_call_target="tpu_custom_call" | custom-call | tf_op jit(solution)/shard_map/fused_layer/pallas_call | solution.py:297
  31.1 0.7 %copy.11 = bf16[1,128,1024]{2,1,0:T(8,128)(2,1)} copy(bf16[1,128,1024]{2,1,0:T(8,128)(2,1)S(1)} %bitcast.9) | data formatting | bytes 524288
  31.8 0.8 %copy.12 = f32[1,1,512,2,128]{4,3,2,1,0:T(2,128)} copy(f32[1,1,512,2,128]{4,3,2,1,0:T(2,128)S(1)} %bitcast.8) | data formatting | bytes 1048576
